TPU v7x, 512 devices: a whole 4x4x16 slice. The times are simulated.
512 devices in a mesh: expert: 8 (over y, x_lo), dp: 64 (over z, x_hi, core).
Axes of the slice: x: 4 (x_hi: 2, x_lo: 2; x = x_hi * 2 + x_lo), y: 4, z: 16, core: 2. Of those that a mesh axis runs over, the one named last changes fastest.
Arguments:
- x_new: bfloat16 [512, 4096], P('expert', 'dp'), may hold values from -6 to 6
- routes_new: int32 [512, 2], P('expert'), may hold values from 0 to 7, all different within a row; in each aligned block of 64 rows (0 to 63, 64 to 127, ...) at most 32 rows name the same one
- gates_new: float32 [512, 2], P('expert'), may hold values from 0.2 to 1
- w_gate: bfloat16 [8, 4096, 7168], P('expert', None, 'dp'), may hold values from -0.09375 to 0.09375
- w_up: bfloat16 [8, 4096, 7168], P('expert', None, 'dp'), may hold values from -0.09375 to 0.09375
- w_down: bfloat16 [8, 7168, 4096], P('expert', 'dp'), may hold values from -0.1875 to 0.1875
- grad_out: bfloat16 [1024, 4096], P('expert', 'dp'), may hold values from -6 to 6
- routes_old: int32 [1024, 2], P('expert'), may hold values from 0 to 7, all different within a row; in each aligned block of 128 rows (0 to 127, 128 to 255, ...) at most 64 rows name the same one
- gates_old: float32 [1024, 2], P('expert'), may hold values from 0.2 to 1
- pre_gate: bfloat16 [8, 512, 7168], P('expert', None, 'dp'), may hold values from -8 to 8
- pre_up: bfloat16 [8, 512, 7168], P('expert', None, 'dp'), may hold values from -6 to 6
Outputs:
- mixed: bfloat16 [512, 4096], P('expert', 'dp')
- grad_down: bfloat16 [8, 7168, 4096], P('expert', 'dp')
- grad_gate: bfloat16 [8, 512, 7168], P('expert', None, 'dp')
- grad_up: bfloat16 [8, 512, 7168], P('expert', None, 'dp')
Inputs may be any that keep to these rules, and one draw needn't show every extreme that they name: `routes_new`: in each group of 64 tokens each expert is named by at most 32 tokens, and by exactly 32 tokens in some group; the two experts of a token differ. `routes_old`: in each group of 128 tokens each expert is named by at most 64 tokens, and by exactly 64 tokens in some group; the two experts of a token differ.
All inputs are finite; a program needn't handle non-finite values.
Results may differ from a plain program's by a relative error of at most 0.0078.
Values may be sent and summed in bfloat16 or wider, within the bound.
No kernel may reach another device: no remote copies, remote signals or barrier semaphores. Data moves between devices by JAX's collectives and lax.ppermute only.
A program may use at most 64 MiB of HBM per device.

v0:
```python
import jax
import jax.numpy as jnp
from jax import lax
from jax.sharding import Mesh
from jax.sharding import PartitionSpec as P

CAP_B = 32
CAP_A = 64
EXPERT = ("expert_0", "expert_1")
DP = ("dp_0", "dp_1", "dp_2")


def split_up(array, dim, size):
    before, after = (array.shape[:dim], array.shape[dim + 1 :])
    return jnp.moveaxis(array.reshape(*before, size, -1, *after), dim, 0)


def in_order(parts, dim):
    parts = jnp.moveaxis(parts, 0, dim)
    shape = parts.shape
    return parts.reshape(*shape[:dim], shape[dim] * shape[dim + 1], *shape[dim + 2 :])


def turned_blocks(parts, axes, turns):
    shape = [lax.axis_size(a) for a in axes]
    parts = parts.reshape(*shape, *parts.shape[1:])
    for k in turns:
        parts = lax.all_to_all(parts, axes[k], split_axis=k, concat_axis=k, tiled=True)
    return parts.reshape(-1, *parts.shape[len(axes) :])


def stepwise_exchange(array, axes, turns, split_dim, concat_dim):
    parts = split_up(array, split_dim, lax.axis_size(axes))
    return in_order(turned_blocks(parts, axes, turns), concat_dim)


def sum_at_owner(array, axis, dim):
    parts = split_up(array, dim, lax.axis_size(axis))
    arrived = lax.all_to_all(parts, axis, split_axis=0, concat_axis=0, tiled=True)
    return arrived.astype(jnp.float32).sum(axis=0)


def gather_in_order(array, axes, turns):
    parts = array[None]
    for k in turns:
        parts = lax.all_gather(parts, axes[k], axis=0, tiled=True)
    current = [lax.axis_size(axes[k]) for k in reversed(turns)]
    parts = parts.reshape(*current, *array.shape)
    turned = sorted(range(len(turns)), key=lambda place: turns[len(turns) - 1 - place])
    return parts.transpose(*turned, *range(len(turns), parts.ndim)).reshape(-1, *array.shape)


def gather_axes(array, axes, turns, dim):
    return in_order(gather_in_order(array, axes, turns), dim)


def slot_table(routes, capacity, experts):
    pairs = routes.reshape(-1)
    onehot = (pairs[:, None] == jnp.arange(experts, dtype=jnp.int32)[None, :]).astype(jnp.int32)
    before = jnp.cumsum(onehot, axis=0) - onehot
    slot = jnp.sum(before * onehot, axis=1)
    column = pairs * capacity + slot
    table = (jnp.arange(experts * capacity, dtype=jnp.int32)[:, None] == column[None, :]).astype(
        jnp.float32
    )
    return table.reshape(experts * capacity, routes.shape[0], 2)


def per_device(
    x_new,
    routes_new,
    gates_new,
    w_gate,
    w_up,
    w_down,
    grad_out,
    routes_old,
    gates_old,
    pre_gate,
    pre_up,
):
    experts = lax.axis_size(EXPERT)
    slice_width = x_new.shape[1]
    gate_weight = w_gate[0]
    up_weight = w_up[0]
    down_weight = w_down[0]
    rows_new = experts * CAP_B
    rows_old = experts * CAP_A
    table_new = slot_table(routes_new, CAP_B, experts)
    picks = jnp.sum(table_new, axis=2).astype(jnp.bfloat16)
    outgoing = jnp.dot(picks, x_new, preferred_element_type=jnp.float32).astype(jnp.bfloat16)
    arrived = stepwise_exchange(outgoing.reshape(experts, CAP_B, slice_width), EXPERT, (0, 1), 0, 0)
    arrived = arrived.reshape(rows_new, slice_width)
    piece = lax.all_gather(arrived, DP, axis=1, tiled=True)
    gate_pre = jnp.dot(piece, gate_weight, preferred_element_type=jnp.float32)
    up_pre = jnp.dot(piece, up_weight, preferred_element_type=jnp.float32)
    hidden = (jax.nn.silu(gate_pre) * up_pre).astype(jnp.bfloat16)
    partial_value = jnp.dot(hidden, down_weight, preferred_element_type=jnp.float32)
    result = sum_at_owner(partial_value.astype(jnp.bfloat16), DP, 1).astype(jnp.bfloat16)
    returned = lax.all_to_all(
        result.reshape(experts, CAP_B, slice_width), EXPERT, split_axis=0, concat_axis=0, tiled=True
    )
    returned = returned.reshape(rows_new, slice_width)
    weights_new = jnp.sum(table_new * gates_new[None, :, :], axis=2)
    mixed = jnp.dot(
        weights_new.T, returned.astype(jnp.float32), precision=lax.Precision.HIGHEST
    ).astype(jnp.bfloat16)
    table_old = slot_table(routes_old, CAP_A, experts)
    weights_old = jnp.sum(table_old * gates_old[None, :, :], axis=2)
    cotangent = jnp.dot(
        weights_old, grad_out.astype(jnp.float32), precision=lax.Precision.HIGHEST
    ).astype(jnp.bfloat16)
    landed = stepwise_exchange(cotangent.reshape(experts, CAP_A, slice_width), EXPERT, (0, 1), 0, 0)
    landed = landed.reshape(rows_old, slice_width)
    saved_gate = pre_gate[0].astype(jnp.float32)
    saved_up = pre_up[0].astype(jnp.float32)
    sigma = jax.nn.sigmoid(saved_gate)
    active = saved_gate * sigma
    hidden_old = (active * saved_up).astype(jnp.bfloat16)
    piece = gather_axes(landed, DP, (1, 0, 2), 1)
    grad_hidden = lax.dot_general(
        piece, down_weight, (((1,), (1,)), ((), ())), preferred_element_type=jnp.float32
    )
    block = lax.dot_general(
        hidden_old, piece, (((0,), (0,)), ((), ())), preferred_element_type=jnp.float32
    )
    weight_grad = block
    grad_hidden, weight_grad = (grad_hidden, weight_grad)
    gate_grad = (grad_hidden * saved_up * sigma * (1.0 + saved_gate * (1.0 - sigma))).astype(
        jnp.bfloat16
    )
    up_grad = (grad_hidden * active).astype(jnp.bfloat16)
    return (mixed, weight_grad.astype(jnp.bfloat16)[None], gate_grad[None], up_grad[None])


def solution(mesh):
    torus = Mesh(
        mesh.devices.reshape(4, 2, 16, 2, 2), ("expert_0", "expert_1", "dp_0", "dp_1", "dp_2")
    )
    placed = (
        P(EXPERT, DP),
        P(EXPERT, None),
        P(EXPERT, None),
        P(EXPERT, None, DP),
        P(EXPERT, None, DP),
        P(EXPERT, DP, None),
        P(EXPERT, DP),
        P(EXPERT, None),
        P(EXPERT, None),
        P(EXPERT, None, DP),
        P(EXPERT, None, DP),
    )
    return jax.shard_map(
        per_device,
        mesh=torus,
        in_specs=placed,
        out_specs=(P(EXPERT, DP), P(EXPERT, DP, None), P(EXPERT, None, DP), P(EXPERT, None, DP)),
        check_vma=False,
    )
```

profile of v0, /device:TPU:1, one launch (start us, length us, event | category | flops | bytes accessed | tf_op | source)
XLA Modules:
  0.0 352.6 jit_solution(8660613464620570664)
XLA Ops:
  7.2 0.8 copy.102
  9.6 0.8 convert_reduce_fusion
  10.4 0.9 convolution_convert_fusion.3
  11.5 9.1 %all_to_all.30 = bf16[4,2,2048]{2,1,0:T(2,128)(2,1)S(1)} all-to-all(bf16[4,2,2048]{2,1,0:T(2,128)(2,1)S(1)} %reshape.97), channel_id=1, replica_groups=mesh['expert_0'=4,'expert_1'=2,'dp_0'=16,'dp_1'=2,'dp_2'=2] {'expert_0'}, dimensions={0} | all-to-all | bytes 65536 | tf_op jit(solution)/shard_map/all_to_all | solution.py:28
  20.9 5.2 %all_to_all.31 = bf16[2,2,4096]{2,1,0:T(2,128)(2,1)S(1)} all-to-all(bf16[2,2,4096]{2,1,0:T(2,128)(2,1)S(1)} %reshape.99), channel_id=1, replica_groups=mesh['expert_0'=4,'expert_1'=2,'dp_0'=16,'dp_1'=2,'dp_2'=2] {'expert_1'}, dimensions={0} | all-to-all | bytes 65536 | tf_op jit(solution)/shard_map/all_to_all | solution.py:28
  27.0 0.8 copy.111
  29.9 0.8 select_reduce_fusion
  31.4 6.8 %all_to_all.32 = bf16[4,2,4096]{2,1,0:T(2,128)(2,1)S(1)} all-to-all(bf16[4,2,4096]{2,1,0:T(2,128)(2,1)S(1)} %reshape.103), channel_id=1, replica_groups=mesh['expert_0'=4,'expert_1'=2,'dp_0'=16,'dp_1'=2,'dp_2'=2] {'expert_0'}, dimensions={0} | all-to-all | bytes 131072 | tf_op jit(solution)/shard_map/all_to_all | solution.py:28
  38.6 5.4 %all_to_all.33 = bf16[2,2,8192]{2,1,0:T(2,128)(2,1)S(1)} all-to-all(bf16[2,2,8192]{2,1,0:T(2,128)(2,1)S(1)} %reshape.105), channel_id=1, replica_groups=mesh['expert_0'=4,'expert_1'=2,'dp_0'=16,'dp_1'=2,'dp_2'=2] {'expert_1'}, dimensions={0} | all-to-all | bytes 131072 | tf_op jit(solution)/shard_map/all_to_all | solution.py:28
  44.4 5.7 %all_gather.13 = bf16[2,512,64]{1,2,0:T(8,128)(2,1)} all-gather(bf16[1,512,64]{1,2,0:T(8,128)(2,1)S(1)} %broadcast_in_dim_reshape_reshape_reshape.3), channel_id=1, replica_groups=mesh['expert_0'=4,'expert_1'=2,'dp_0'=16,'dp_1'=2,'dp_2'=2] {'dp_1'}, dimensions={0}, use_global_device_ids=true | all-gather | bytes 196608 | tf_op jit(solution)/shard_map/all_gather | solution.py:46
  50.2 126.3 %all-gather.4.cloned.1.call-done = bf16[256,4096]{0,1:T(8,128)(2,1)} async-done(((bf16[256,64]{0,1:T(8,128)(2,1)}), bf16[256,4096]{0,1:T(8,128)(2,1)}) %all-gather.4.cloned.1.call-update) | async-done | bytes 2097168 | tf_op jit(solution)/shard_map/all_gather | solution.py:94
  176.4 2.5 fusion.7
  178.9 4.2 %convolution_convert_fusion = bf16[256,4096]{1,0:T(8,128)(2,1)} fusion(bf16[256,4096]{0,1:T(8,128)(2,1)S(1)} %copy-done.2, bf16[1,112,4096]{2,1,0:T(8,128)(2,1)S(1)} %copy-done, bf16[1,4096,112]{1,2,0:T(8,128)(2,1)} %param.15, f32[256,112]{0,1:T(8,128)S(1)} %fusion.7), kind=kOutput, calls=%fused_computation | convolution fusion | flops 470982656 | bytes 6144000 | tf_op jit(solution)/shard_map/dot_general | solution.py:98
  183.1 4.1 %copy.109 = bf16[256,4096]{0,1:T(8,128)(2,1)} copy(bf16[256,4096]{1,0:T(8,128)(2,1)} %convolution_convert_fusion) | data formatting | bytes 4194304 | tf_op jit(solution)/shard_map/convert_element_type | solution.py:99
  187.2 7.9 %all-to-all-start.2 = ((bf16[64,256,64]{1,2,0:T(8,128)(2,1)}), bf16[64,256,64]{1,2,0:T(8,128)(2,1)S(1)}, u32[]{:S(2)}, u32[]{:S(2)}) async-start(bf16[64,256,64]{1,2,0:T(8,128)(2,1)} %bitcast.121), calls=%async_computation.2 | async-start | bytes 4194304 | tf_op jit(solution)/shard_map/all_to_all | solution.py:39
  195.1 102.4 %all-gather.6.cloned.1.call-done = bf16[32,512,64]{1,2,0:T(8,128)(2,1)} async-done(((bf16[2,512,64]{1,2,0:T(8,128)(2,1)}), bf16[32,512,64]{1,2,0:T(8,128)(2,1)}) %all-gather.6.cloned.1.call-update) | async-done | bytes 2097168 | tf_op jit(solution)/shard_map/all_gather | solution.py:46
  297.6 31.2 %all-gather.8.cloned.1.call-done = bf16[64,512,64]{1,2,0:T(8,128)(2,1)} async-done(((bf16[32,512,64]{1,2,0:T(8,128)(2,1)}), bf16[64,512,64]{1,2,0:T(8,128)(2,1)}) %all-gather.8.cloned.1.call-update) | async-done | bytes 4194320 | tf_op jit(solution)/shard_map/all_gather | solution.py:46
  328.8 2.7 copy.117
  331.6 1.9 copy-done.1
  333.5 1.5 fusion.33
  335.4 0.7 reshape.101
  336.1 3.9 %all-to-all-start.3 = ((bf16[8,2,1024]{2,1,0:T(2,128)(2,1)}), bf16[8,2,1024]{2,1,0:T(2,128)(2,1)S(1)}, u32[]{:S(2)}, u32[]{:S(2)}) async-start(bf16[8,2,1024]{2,1,0:T(2,128)(2,1)} %reshape.101), calls=%async_computation.3 | async-start | bytes 65536 | tf_op jit(solution)/shard_map/all_to_all | solution.py:100
  340.0 4.5 %fusion = bf16[1,112,4096]{2,1,0:T(8,128)(2,1)} fusion(bf16[512,4096]{0,1:T(8,128)(2,1)} %bitcast.120, bf16[1,512,112]{1,2,0:T(8,128)(2,1)S(1)} %copy-done.3, bf16[1,512,112]{1,2,0:T(8,128)(2,1)S(1)} %copy-done.4), kind=kOutput, calls=%fused_computation.2 | convolution fusion | flops 470679552 | bytes 5341184 | tf_op jit(solution)/shard_map/dot_general | solution.py:124
  345.2 0.8 convolution_convert_fusion.4
  (58 shorter events, 7.7 us)
Async XLA Ops:
  7.2 171.7 %copy-start = (bf16[1,112,4096]{2,1,0:T(8,128)(2,1)S(1)}, bf16[1,112,4096]{2,1,0:T(8,128)(2,1)}, u32[]{:S(2)}) copy-start(bf16[1,112,4096]{2,1,0:T(8,128)(2,1)} %param.16) | copy-start | bytes 2752516
  7.2 23.5 %copy-start.5 = (bf16[128,64]{0,1:T(8,128)(2,1)S(1)}, bf16[128,64]{0,1:T(8,128)(2,1)}, u32[]{:S(2)}) copy-start(bf16[128,64]{0,1:T(8,128)(2,1)} %param.17) | copy-start | bytes 49156
  7.2 169.2 %all-gather.4.cloned.1.call-start = ((), (), s32[]{:S(2)}) async-start(), calls=%async_computation.6 | async-start | bytes 2129920 | tf_op jit(solution)/shard_map/all_gather | solution.py:94
  26.9 270.7 %all-gather.6.cloned.1.call-start = ((), (), s32[]{:S(2)}) async-start(), calls=%async_computation.7 | async-start | bytes 2228224 | tf_op jit(solution)/shard_map/all_gather | solution.py:46
  176.4 2.5 copy-start.2
  187.2 147.8 %all-to-all-start.2 = ((bf16[64,256,64]{1,2,0:T(8,128)(2,1)}), bf16[64,256,64]{1,2,0:T(8,128)(2,1)S(1)}, u32[]{:S(2)}, u32[]{:S(2)}) async-start(bf16[64,256,64]{1,2,0:T(8,128)(2,1)} %bitcast.121), calls=%async_computation.2 | async-start | bytes 4194304 | tf_op jit(solution)/shard_map/all_to_all | solution.py:39
  195.1 133.7 %all-gather.8.cloned.1.call-start = ((), (), s32[]{:S(2)}) async-start(), calls=%async_computation.8 | async-start | bytes 6291456 | tf_op jit(solution)/shard_map/all_gather | solution.py:46
  328.8 4.7 %copy-start.3 = (bf16[1,512,112]{1,2,0:T(8,128)(2,1)S(1)}, bf16[1,512,112]{1,2,0:T(8,128)(2,1)}, u32[]{:S(2)}) copy-start(bf16[1,512,112]{1,2,0:T(8,128)(2,1)} %param.21) | copy-start | bytes 344068
  328.8 4.7 %copy-start.4 = (bf16[1,512,112]{1,2,0:T(8,128)(2,1)S(1)}, bf16[1,512,112]{1,2,0:T(8,128)(2,1)}, u32[]{:S(2)}) copy-start(bf16[1,512,112]{1,2,0:T(8,128)(2,1)} %param.20) | copy-start | bytes 344068
  331.6 1.9 copy-start.1
  336.1 9.0 %all-to-all-start.3 = ((bf16[8,2,1024]{2,1,0:T(2,128)(2,1)}), bf16[8,2,1024]{2,1,0:T(2,128)(2,1)S(1)}, u32[]{:S(2)}, u32[]{:S(2)}) async-start(bf16[8,2,1024]{2,1,0:T(2,128)(2,1)} %reshape.101), calls=%async_computation.3 | async-start | bytes 65536 | tf_op jit(solution)/shard_map/all_to_all | solution.py:100
Sparse Core Ops, SparseCore 0:
  27.0 149.3 all-gather.3
  178.5 119.0 all-gather.5
  299.7 29.1 all-gather.7
where the time goes:
time: 353 us
  waiting for transfers between devices  261 us (74%)
  blocking collectives  32.2 us (9%)
  local copies, waits for them, and re-layouts  14.9 us (4%)
  matrix products  14.6 us (4%)
  between operations  14 us (4%)
  starting transfers between devices  11.9 us (3%)
  other arithmetic  4.41 us (1%)
    all_gather x2, waiting for transfers between devices, gather_in_order(): parts = lax.all_gather(parts, axes[k], axis=0, tiled=True)  134 us
    all_gather x1, waiting for transfers between devices, per_device(): piece = lax.all_gather(arrived, DP, axis=1, tiled=True)  126 us
    all_to_all x4, blocking collectives, turned_blocks(): lax.all_to_all(parts, axes[k], split_axis=k, concat_axis=k, tiled=True)  26.5 us
    all_to_all x1, starting transfers between devices, sum_at_owner(): lax.all_to_all(parts, axis, split_axis=0, concat_axis=0, tiled=True)  7.87 us
  transfers between devices with their start and end apart: 5, of which 4 were waited for; matrix products, arithmetic and copies ran while one was open for 7% of the time, Pallas kernels for 0%

commit v1 on v0

--- a/solution.py
+++ b/solution.py
@@ -91,7 +91,9 @@
     outgoing = jnp.dot(picks, x_new, preferred_element_type=jnp.float32).astype(jnp.bfloat16)
     arrived = stepwise_exchange(outgoing.reshape(experts, CAP_B, slice_width), EXPERT, (0, 1), 0, 0)
     arrived = arrived.reshape(rows_new, slice_width)
-    piece = lax.all_gather(arrived, DP, axis=1, tiled=True)
+    piece = jnp.concatenate(
+        lax.all_to_all(jnp.stack([arrived] * lax.axis_size(DP)), DP, 0, 0), axis=1
+    )
     gate_pre = jnp.dot(piece, gate_weight, preferred_element_type=jnp.float32)
     up_pre = jnp.dot(piece, up_weight, preferred_element_type=jnp.float32)
     hidden = (jax.nn.silu(gate_pre) * up_pre).astype(jnp.bfloat16)

time: 353 us -> 321 us (0.909); the launches traced: 353 us -> 317 us
  waiting for transfers between devices: 261 us -> 209 us
  starting transfers between devices: 11.9 us -> 49.7 us
  blocking collectives: 32.2 us -> 6.25 us
    all_gather x1 -> x0, waiting for transfers between devices: 126 us -> none  [per_device(): piece = lax.all_gather(arrived, DP, axis=1, tiled=True)]
    all_to_all x0 -> x5, waiting for transfers between devices: none -> 117 us  [the longest x1 108 us: per_device(): lax.all_to_all(jnp.stack([arrived] * lax.axis_size(DP)), DP, 0, 0)]
    all_gather x2, waiting for transfers between devices: 134 us -> 26 us  [gather_in_order(): parts = lax.all_gather(parts, axes[k], axis=0, tiled=True)]
    all_to_all x1, waiting for transfers between devices: 0.01 us -> 65.5 us  [sum_at_owner(): lax.all_to_all(parts, axis, split_axis=0, concat_axis=0, tiled=True)]
    all_to_all x0 -> x5, starting transfers between devices: none -> 38.6 us  [the longest x1 22.8 us: per_device(): lax.all_to_all(jnp.stack([arrived] * lax.axis_size(DP)), DP, 0, 0)]
    all_to_all x4 -> x0, blocking collectives: 26.5 us -> none  [turned_blocks(): lax.all_to_all(parts, axes[k], split_axis=k, concat_axis=k, tiled=True)]
    unnamed x25 -> x21, local copies, waits for them, and re-layouts: 5.5 us -> 7.98 us
  transfers between devices with their start and end apart: 5 -> 9, of which waited for: 4 -> 7; matrix products, arithmetic and copies ran while one was open for 7% -> 8% of each run, Pallas kernels for 0% -> 0%
where the time goes in v1:
time: 321 us; the launch traced here: 317 us
  waiting for transfers between devices  209 us (65%)
  starting transfers between devices  49.7 us (15%)
  local copies, waits for them, and re-layouts  18.4 us (6%)
  matrix products  14.5 us (5%)
  between operations  14.3 us (4%)
  blocking collectives  6.25 us (2%)
  other arithmetic  4.41 us (1%)
    all_to_all x1, waiting for transfers between devices, per_device(): lax.all_to_all(jnp.stack([arrived] * lax.axis_size(DP)), DP, 0, 0)  108 us
    all_to_all x1, waiting for transfers between devices, sum_at_owner(): lax.all_to_all(parts, axis, split_axis=0, concat_axis=0, tiled=True)  65.5 us
    all_gather x2, waiting for transfers between devices, gather_in_order(): parts = lax.all_gather(parts, axes[k], axis=0, tiled=True)  26 us
    all_to_all x1, starting transfers between devices, per_device(): lax.all_to_all(jnp.stack([arrived] * lax.axis_size(DP)), DP, 0, 0)  22.8 us
    all_to_all x4, starting transfers between devices, turned_blocks(): lax.all_to_all(parts, axes[k], split_axis=k, concat_axis=k, tiled=True)  15.8 us
    all_to_all x4, waiting for transfers between devices, turned_blocks(): lax.all_to_all(parts, axes[k], split_axis=k, concat_axis=k, tiled=True)  8.37 us
    unnamed x21, local copies, waits for them, and re-layouts  7.98 us
    all_to_all x1, starting transfers between devices, sum_at_owner(): lax.all_to_all(parts, axis, split_axis=0, concat_axis=0, tiled=True)  7.67 us
  transfers between devices with their start and end apart: 9, of which 7 were waited for; matrix products, arithmetic and copies ran while one was open for 8% of the time, Pallas kernels for 0%

profile of v1, /device:TPU:1, one launch (start us, length us, event | category | flops | bytes accessed | tf_op | source)
XLA Modules:
  0.0 316.8 jit_solution(5156740645625930066)
XLA Ops:
  10.3 0.9 convolution_convert_fusion.3
  12.1 5.0 %all-to-all-start = ((bf16[4,2,2048]{2,1,0:T(2,128)(2,1)}), bf16[4,2,2048]{2,1,0:T(2,128)(2,1)S(1)}, u32[]{:S(2)}, u32[]{:S(2)}) async-start(bf16[4,2,2048]{2,1,0:T(2,128)(2,1)} %reshape.107), calls=%async_computation | async-start | bytes 65536 | tf_op jit(solution)/shard_map/all_to_all | solution.py:28
  20.8 1.0 convolution_convert_fusion.2
  22.9 4.2 %all-to-all-start.5 = ((bf16[4,2,4096]{2,1,0:T(2,128)(2,1)}), bf16[4,2,4096]{2,1,0:T(2,128)(2,1)S(1)}, u32[]{:S(2)}, u32[]{:S(2)}) async-start(bf16[4,2,4096]{2,1,0:T(2,128)(2,1)} %reshape.113), calls=%async_computation.5 | async-start | bytes 131072 | tf_op jit(solution)/shard_map/all_to_all | solution.py:28
  28.0 3.6 %all-to-all-done.5 = bf16[4,2,4096]{2,1,0:T(2,128)(2,1)S(1)} async-done(((bf16[4,2,4096]{2,1,0:T(2,128)(2,1)}), bf16[4,2,4096]{2,1,0:T(2,128)(2,1)S(1)}, u32[]{:S(2)}, u32[]{:S(2)}) %all-to-all-start.5) | async-done | bytes 65568 | tf_op jit(solution)/shard_map/all_to_all | solution.py:28
  31.6 3.3 %all-to-all-start.1 = ((bf16[2,2,4096]{2,1,0:T(2,128)(2,1)}), bf16[2,2,4096]{2,1,0:T(2,128)(2,1)S(1)}, u32[]{:S(2)}, u32[]{:S(2)}) async-start(bf16[2,2,4096]{2,1,0:T(2,128)(2,1)} %reshape.109), calls=%async_computation.1 | async-start | bytes 65536 | tf_op jit(solution)/shard_map/all_to_all | solution.py:28
  35.9 2.0 all-to-all-done.1
  37.9 3.3 %all-to-all-start.6 = ((bf16[2,2,8192]{2,1,0:T(2,128)(2,1)}), bf16[2,2,8192]{2,1,0:T(2,128)(2,1)S(1)}, u32[]{:S(2)}, u32[]{:S(2)}) async-start(bf16[2,2,8192]{2,1,0:T(2,128)(2,1)} %reshape.115), calls=%async_computation.6 | async-start | bytes 131072 | tf_op jit(solution)/shard_map/all_to_all | solution.py:28
  41.4 2.7 all-to-all-done.6
  44.2 1.6 stack.3
  45.8 22.8 %all-to-all-start.2 = ((bf16[64,256,64]{1,2,0:T(8,128)(2,1)}), bf16[64,256,64]{1,2,0:T(8,128)(2,1)S(1)}, u32[]{:S(2)}, u32[]{:S(2)}) async-start(bf16[64,256,64]{1,2,0:T(8,128)(2,1)} %stack.3), calls=%async_computation.2 | async-start | bytes 4194304 | tf_op jit(solution)/shard_map/all_to_all | solution.py:95
  69.0 6.3 %all_gather.9 = bf16[2,512,64]{1,2,0:T(8,128)(2,1)} all-gather(bf16[1,512,64]{1,2,0:T(8,128)(2,1)S(1)} %broadcast_in_dim_reshape_reshape_reshape.3), channel_id=1, replica_groups=mesh['expert_0'=4,'expert_1'=2,'dp_0'=16,'dp_1'=2,'dp_2'=2] {'dp_1'}, dimensions={0}, use_global_device_ids=true | all-gather | bytes 196608 | tf_op jit(solution)/shard_map/all_gather | solution.py:46
  75.3 108.2 %all-to-all-done.2 = bf16[64,256,64]{1,2,0:T(8,128)(2,1)S(1)} async-done(((bf16[64,256,64]{1,2,0:T(8,128)(2,1)}), bf16[64,256,64]{1,2,0:T(8,128)(2,1)S(1)}, u32[]{:S(2)}, u32[]{:S(2)}) %all-to-all-start.2) | async-done | bytes 2097184 | tf_op jit(solution)/shard_map/all_to_all | solution.py:95
  183.6 1.6 fusion.7
  185.2 4.2 %convolution_convert_fusion = bf16[256,4096]{1,0:T(8,128)(2,1)} fusion(bf16[256,4096]{0,1:T(8,128)(2,1)S(1)} %bitcast.123, bf16[1,112,4096]{2,1,0:T(8,128)(2,1)S(1)} %copy-done, bf16[1,4096,112]{1,2,0:T(8,128)(2,1)} %param.15, f32[256,112]{0,1:T(8,128)S(1)} %fusion.7), kind=kOutput, calls=%fused_computation | convolution fusion | flops 470982656 | bytes 6144000 | tf_op jit(solution)/shard_map/dot_general | solution.py:100
  189.4 4.1 %copy.112 = bf16[256,4096]{0,1:T(8,128)(2,1)} copy(bf16[256,4096]{1,0:T(8,128)(2,1)} %convolution_convert_fusion) | data formatting | bytes 4194304 | tf_op jit(solution)/shard_map/convert_element_type | solution.py:101
  193.5 7.7 %all-to-all-start.3 = ((bf16[64,256,64]{1,2,0:T(8,128)(2,1)}), bf16[64,256,64]{1,2,0:T(8,128)(2,1)S(1)}, u32[]{:S(2)}, u32[]{:S(2)}) async-start(bf16[64,256,64]{1,2,0:T(8,128)(2,1)} %bitcast.126), calls=%async_computation.3 | async-start | bytes 4194304 | tf_op jit(solution)/shard_map/all_to_all | solution.py:39
  201.9 26.0 %all-gather.5.cloned.1.call-done = bf16[64,512,64]{1,2,0:T(8,128)(2,1)} async-done(((bf16[32,512,64]{1,2,0:T(8,128)(2,1)}), bf16[64,512,64]{1,2,0:T(8,128)(2,1)}) %all-gather.5.cloned.1.call-update) | async-done | bytes 4194320 | tf_op jit(solution)/shard_map/all_gather | solution.py:46
  227.9 2.7 copy.120
  230.6 1.9 copy-done.1
  232.6 1.5 fusion.33
  234.0 65.5 %all-to-all-done.3 = bf16[64,256,64]{1,2,0:T(8,128)(2,1)S(1)} async-done(((bf16[64,256,64]{1,2,0:T(8,128)(2,1)}), bf16[64,256,64]{1,2,0:T(8,128)(2,1)S(1)}, u32[]{:S(2)}, u32[]{:S(2)}) %all-to-all-start.3) | async-done | bytes 2097184 | tf_op jit(solution)/shard_map/all_to_all | solution.py:39
  300.7 3.3 %all-to-all-start.4 = ((bf16[8,2,1024]{2,1,0:T(2,128)(2,1)}), bf16[8,2,1024]{2,1,0:T(2,128)(2,1)S(1)}, u32[]{:S(2)}, u32[]{:S(2)}) async-start(bf16[8,2,1024]{2,1,0:T(2,128)(2,1)} %reshape.111), calls=%async_computation.4 | async-start | bytes 65536 | tf_op jit(solution)/shard_map/all_to_all | solution.py:102
  304.0 4.5 %fusion = bf16[1,112,4096]{2,1,0:T(8,128)(2,1)} fusion(bf16[512,4096]{0,1:T(8,128)(2,1)} %bitcast.125, bf16[1,512,112]{1,2,0:T(8,128)(2,1)S(1)} %copy-done.2, bf16[1,512,112]{1,2,0:T(8,128)(2,1)S(1)} %copy-done.3), kind=kOutput, calls=%fused_computation.2 | convolution fusion | flops 470679552 | bytes 5341184 | tf_op jit(solution)/shard_map/dot_general | solution.py:126
  (58 shorter events, 14.5 us)
Async XLA Ops:
  7.2 178.0 %copy-start = (bf16[1,112,4096]{2,1,0:T(8,128)(2,1)S(1)}, bf16[1,112,4096]{2,1,0:T(8,128)(2,1)}, u32[]{:S(2)}) copy-start(bf16[1,112,4096]{2,1,0:T(8,128)(2,1)} %param.16) | copy-start | bytes 2752516
  12.1 10.7 %all-to-all-start = ((bf16[4,2,2048]{2,1,0:T(2,128)(2,1)}), bf16[4,2,2048]{2,1,0:T(2,128)(2,1)S(1)}, u32[]{:S(2)}, u32[]{:S(2)}) async-start(bf16[4,2,2048]{2,1,0:T(2,128)(2,1)} %reshape.107), calls=%async_computation | async-start | bytes 65536 | tf_op jit(solution)/shard_map/all_to_all | solution.py:28
  22.9 8.7 %all-to-all-start.5 = ((bf16[4,2,4096]{2,1,0:T(2,128)(2,1)}), bf16[4,2,4096]{2,1,0:T(2,128)(2,1)S(1)}, u32[]{:S(2)}, u32[]{:S(2)}) async-start(bf16[4,2,4096]{2,1,0:T(2,128)(2,1)} %reshape.113), calls=%async_computation.5 | async-start | bytes 131072 | tf_op jit(solution)/shard_map/all_to_all | solution.py:28
  31.6 6.3 %all-to-all-start.1 = ((bf16[2,2,4096]{2,1,0:T(2,128)(2,1)}), bf16[2,2,4096]{2,1,0:T(2,128)(2,1)S(1)}, u32[]{:S(2)}, u32[]{:S(2)}) async-start(bf16[2,2,4096]{2,1,0:T(2,128)(2,1)} %reshape.109), calls=%async_computation.1 | async-start | bytes 65536 | tf_op jit(solution)/shard_map/all_to_all | solution.py:28
  37.9 6.3 %all-to-all-start.6 = ((bf16[2,2,8192]{2,1,0:T(2,128)(2,1)}), bf16[2,2,8192]{2,1,0:T(2,128)(2,1)S(1)}, u32[]{:S(2)}, u32[]{:S(2)}) async-start(bf16[2,2,8192]{2,1,0:T(2,128)(2,1)} %reshape.115), calls=%async_computation.6 | async-start | bytes 131072 | tf_op jit(solution)/shard_map/all_to_all | solution.py:28
  45.8 137.8 %all-to-all-start.2 = ((bf16[64,256,64]{1,2,0:T(8,128)(2,1)}), bf16[64,256,64]{1,2,0:T(8,128)(2,1)S(1)}, u32[]{:S(2)}, u32[]{:S(2)}) async-start(bf16[64,256,64]{1,2,0:T(8,128)(2,1)} %stack.3), calls=%async_computation.2 | async-start | bytes 4194304 | tf_op jit(solution)/shard_map/all_to_all | solution.py:95
  68.6 132.7 %all-gather.3.cloned.1.call-start = ((), (), s32[]{:S(2)}) async-start(), calls=%async_computation.7 | async-start | bytes 2228224 | tf_op jit(solution)/shard_map/all_gather | solution.py:46
  193.5 106.0 %all-to-all-start.3 = ((bf16[64,256,64]{1,2,0:T(8,128)(2,1)}), bf16[64,256,64]{1,2,0:T(8,128)(2,1)S(1)}, u32[]{:S(2)}, u32[]{:S(2)}) async-start(bf16[64,256,64]{1,2,0:T(8,128)(2,1)} %bitcast.126), calls=%async_computation.3 | async-start | bytes 4194304 | tf_op jit(solution)/shard_map/all_to_all | solution.py:39
  201.2 26.7 %all-gather.5.cloned.1.call-start = ((), (), s32[]{:S(2)}) async-start(), calls=%async_computation.8 | async-start | bytes 6291456 | tf_op jit(solution)/shard_map/all_gather | solution.py:46
  227.9 4.7 %copy-start.2 = (bf16[1,512,112]{1,2,0:T(8,128)(2,1)S(1)}, bf16[1,512,112]{1,2,0:T(8,128)(2,1)}, u32[]{:S(2)}) copy-start(bf16[1,512,112]{1,2,0:T(8,128)(2,1)} %param.21) | copy-start | bytes 344068
  227.9 4.7 %copy-start.3 = (bf16[1,512,112]{1,2,0:T(8,128)(2,1)S(1)}, bf16[1,512,112]{1,2,0:T(8,128)(2,1)}, u32[]{:S(2)}) copy-start(bf16[1,512,112]{1,2,0:T(8,128)(2,1)} %param.20) | copy-start | bytes 344068
  230.6 1.9 copy-start.1
  300.7 8.4 %all-to-all-start.4 = ((bf16[8,2,1024]{2,1,0:T(2,128)(2,1)}), bf16[8,2,1024]{2,1,0:T(2,128)(2,1)S(1)}, u32[]{:S(2)}, u32[]{:S(2)}) async-start(bf16[8,2,1024]{2,1,0:T(2,128)(2,1)} %reshape.111), calls=%async_computation.4 | async-start | bytes 65536 | tf_op jit(solution)/shard_map/all_to_all | solution.py:102
Sparse Core Ops, SparseCore 0:
  75.4 114.2 all-gather.2
  204.1 23.7 all-gather.4
